TPU v7x, 128 devices: a whole 4x4x4 slice. The times are simulated.
128 devices in a mesh: blk: 32 (over x, z_hi, y), org: 4 (over z_lo, core).
Axes of the slice: x: 4, y: 4, z: 4 (z_hi: 2, z_lo: 2; z = z_hi * 2 + z_lo), core: 2. Of those that a mesh axis runs over, the one named last changes fastest.
Arguments:
- warm_labels: float32 [256, 512, 1024], P('blk', None, 'org'), may hold values from 0 to 6
- link_costs: float32 [4, 256, 512], P(None, 'blk'), may hold values from 0.05 to 1.5
- anchor_nodes: int32 [1024], P('org'), may hold values from 0 to 131071
- demand: float32 [1024], P('org'), may hold values from 0.2 to 2
Outputs:
- labels: float32 [256, 512, 1024], P('blk', None, 'org')
- link_weights: float32 [4, 256, 512], P(None, 'blk', 'org')
Inputs may be any that keep to these rules, and one draw needn't show every extreme that they name: `anchor_nodes`: node numbers r * 512 + c.
All inputs are finite; a program needn't handle non-finite values.
Results may differ from a plain program's by a relative error of at most 0.0003.
Values sent between devices are 32-bit elements; how exact they have to be, the bound alone decides.
No kernel may reach another device: no remote copies, remote signals or barrier semaphores. Data moves between devices by JAX's collectives and lax.ppermute only.
A program may use at most 128 MiB of HBM per device.

v0:
```python
import functools
import jax
import jax.numpy as jnp
from jax import lax
from jax.experimental import pallas as pl
from jax.experimental.pallas import tpu as pltpu
from jax.sharding import PartitionSpec as P


ANCHORS = 1024
STEPS = 6
EDGE = 6
FIRST = 4
PAD = 8
CH = 128
far_value = 1000000000.0
temper = 0.5
F32 = jnp.float32
WEST, EAST, NORTH, SOUTH = range(4)
OUTER = (NORTH, SOUTH)
INNER_SIDE = (SOUTH, NORTH)


def row_of(side, depth):
    return depth if side == 0 else 7 - depth


def cost_row(side, depth):
    return EDGE + row_of(side, depth)


def chunks(cols, body):
    def step(i, carry):
        body(pl.multiple_of(i * CH, CH))
        return carry

    lax.fori_loop(0, cols // CH, step, 0)


def half_lanes(h):
    return pl.ds(h * 128, 128)


def clear_pads(buf, rows, cols):
    zero = jnp.zeros((PAD, 128), F32)
    for r in range(rows):
        for h in range(2):
            buf[r, h, pl.ds(0, PAD), :] = zero
            buf[r, h, pl.ds(cols + PAD, PAD), :] = zero


def anchored(values, anchors, node0):
    ids = node0 + lax.broadcasted_iota(jnp.int32, values.shape, 0)
    return jnp.where(ids == anchors, 0.0, values)


def add_lane_sum(sums, side, row, piece, terms):
    at = side * 8 + row
    sums[piece, at : at + 1, :] += jnp.sum(terms, axis=1)[None, :]


def spread_kernel(lanes, cols_ref, out_ref, sem):
    cols = cols_ref.shape[0]

    def body(c0):
        block = cols_ref[pl.ds(c0, CH), :]
        for lane in range(lanes):
            out_ref[lane, pl.ds(c0, CH), :] = jnp.broadcast_to(block[:, lane : lane + 1], (CH, 128))

    chunks(cols, body)


def first_kernel(info, own, lead1, lead2, more1, more2, anchors, demand, cost, g_out, d_out, lab_out, sums, labels, buf, sem):
    cols = own.shape[1]
    rows = 8 + 2 * FIRST
    odd = info[1]
    north_of = (odd, 1 - odd)
    loads = []
    for i in range(8):
        loads.append((own, i, FIRST + i))
    for lead, more, north in ((lead1, more1, north_of[0]), (lead2, more2, north_of[1])):
        loads.append((lead, None, FIRST + 8 - north * 9))
        for i in range(FIRST - 1):
            loads.append((more, i, (FIRST + 9) * (1 - north) + i))
    loads = [
        pltpu.make_async_copy(
            ref.at[pl.ds(0, cols), half_lanes(h)] if i is None else ref.at[i, :, half_lanes(h)],
            buf.at[at, h, pl.ds(PAD, cols), :],
            sem.at[n, h],
        )
        for n, (ref, i, at) in enumerate(loads)
        for h in range(2)
    ]
    for copy in loads:
        copy.start()
    sums[...] = jnp.zeros(sums.shape, F32)
    clear_pads(buf, rows, cols)
    for copy in loads:
        copy.wait()

    def mark(i, carry):
        node0 = (info[0] + i - FIRST) * cols

        def body(c0):
            here = pl.ds(c0 + PAD, CH)
            for h in range(2):
                buf[i, h, here, :] = anchored(buf[i, h, here, :], anchors[:, half_lanes(h)], node0 + c0)

        chunks(cols, body)
        return carry

    lax.fori_loop(0, rows, mark, 0)
    for t in range(1, STEPS + 1):
        have = rows - 2 * (t - 1)
        for side in range(2):
            at, inner = (0, 1) if side == 0 else (have - 1, have - 2)
            j = 4 * (row_of(side, t - FIRST - 1) + EDGE)

            def edge(c0, side=side, at=at, inner=inner, j=j, t=t):
                here, mid = pl.ds(c0, CH), pl.ds(c0 + PAD, CH)
                west, east, within = (cost[j + k, here, :] for k in (WEST, EAST, INNER_SIDE[side]))
                for h in range(2):
                    centre = buf[at, h, mid, :]
                    g_out[side * STEPS + t - 1, h, here, :] = jnp.minimum(
                        jnp.minimum(centre, buf[at, h, pl.ds(c0 + PAD - 1, CH), :] + west),
                        jnp.minimum(buf[at, h, pl.ds(c0 + PAD + 1, CH), :] + east, buf[inner, h, mid, :] + within),
                    )
                    d_out[side * STEPS + t - 1, h, here, :] = centre

            chunks(cols, edge)

        def row(i, carry, t=t):
            j = 4 * (i + t - FIRST + EDGE)

            def body(c0):
                here, mid = pl.ds(c0, CH), pl.ds(c0 + PAD, CH)
                west, east, up, down = (cost[j + k, here, :] for k in (WEST, EAST, NORTH, SOUTH))
                for h in range(2):
                    buf[i, h, mid, :] = jnp.minimum(
                        jnp.minimum(
                            jnp.minimum(buf[i + 1, h, mid, :], buf[i + 1, h, pl.ds(c0 + PAD - 1, CH), :] + west),
                            jnp.minimum(buf[i + 1, h, pl.ds(c0 + PAD + 1, CH), :] + east, buf[i, h, mid, :] + up),
                        ),
                        buf[i + 2, h, mid, :] + down,
                    )

            chunks(cols, body)
            return carry

        lax.fori_loop(0, have - 2, row, 0)

    stores = [
        pltpu.make_async_copy(buf.at[r, h, pl.ds(PAD, cols), :], labels.at[r + 2, :, half_lanes(h)], sem.at[r, h])
        for r in range(4)
        for h in range(2)
    ]
    for copy in stores:
        copy.start()
    exps = 8

    def final(c0):
        for r in range(4):
            for h in range(2):
                value = buf[r, h, pl.ds(c0 + PAD, CH), :]
                if r % 3 == 0:
                    lab_out[r // 3, pl.ds(c0, CH), half_lanes(h)] = value
                buf[r + exps, h, pl.ds(c0 + PAD, CH), :] = jnp.exp(-temper * value)

    chunks(cols, final)

    def link(c0):
        piece = c0 // CH
        mid = pl.ds(c0 + PAD, CH)
        for r in range(4):
            inv = [demand[:, half_lanes(h)] * jnp.exp(temper * buf[r, h, mid, :]) for h in range(2)]

            def add(side, shift, other, inv=inv, r=r):
                terms = [inv[h] * buf[other + exps, h, pl.ds(c0 + PAD + shift, CH), :] for h in range(2)]
                add_lane_sum(sums, side, r + 2, piece, terms[0] + terms[1])

            add(WEST, -1, r)
            add(EAST, 1, r)
            if r > 0:
                add(NORTH, 0, r - 1)
            if r < 3:
                add(SOUTH, 0, r + 1)

    chunks(cols, link)
    for copy in stores:
        copy.wait()


def pick(got1, got2, odd, side, here, lanes):
    one, two = got1[0, here, lanes], got2[0, here, lanes]
    return jnp.where(odd, one, two) if side == 0 else jnp.where(odd, two, one)


def put_rows(pairs, sem):
    copies = [pltpu.make_async_copy(src, dst, sem.at[n]) for n, (src, dst) in enumerate(pairs)]
    for copy in copies:
        copy.start()
    for copy in copies:
        copy.wait()


def next_kernel(depth, last, *refs):
    info, got1, got2, anchors, demand, cost, g_in, d_in, in_lab, sums_in, _ = refs[:11]
    if last:
        far_out, lab_out, sums, labels, dbuf, ebuf, sem = refs[11:]
    else:
        g_out, d_out, lab_out, sums, labels, dbuf, ebuf, sem = refs[11:]
    cols = got1.shape[1]
    odd = info[1] > 0
    at_rows = tuple(row_of(side, STEPS - depth) for side in range(2))
    sums[...] = sums_in[...]
    clear_pads(dbuf, STEPS, cols)
    clear_pads(ebuf, 1, cols)
    for side in range(2):
        within = 0 if side == 0 else in_lab.shape[0] - 1
        node0 = (info[0] + row_of(side, -depth)) * cols

        def chain(c0, side=side, node0=node0):
            here, mid = pl.ds(c0, CH), pl.ds(c0 + PAD, CH)
            values = []
            for h in range(2):
                values.append(anchored(pick(got1, got2, odd, side, here, half_lanes(h)), anchors[:, half_lanes(h)], node0 + c0))
                dbuf[0, h, mid, :] = values[h]
            for t in range(1, STEPS + 1):
                outer = cost[4 * cost_row(side, t - depth) + OUTER[side], here, :]
                for h in range(2):
                    values[h] = jnp.minimum(g_in[side * STEPS + t - 1, h, here, :], values[h] + outer)
                    if t < STEPS:
                        dbuf[t, h, mid, :] = values[h]
            for h in range(2):
                lab_out[side, here, half_lanes(h)] = values[h]
                ebuf[0, h, mid, :] = jnp.exp(-temper * values[h])

        chunks(cols, chain)

        def ahead(c0, side=side):
            here, mid = pl.ds(c0, CH), pl.ds(c0 + PAD, CH)
            best = [None, None]
            for t in range(1, STEPS + 1):
                j = 4 * cost_row(side, t - depth - 1)
                west, east, inner = (cost[j + k, here, :] for k in (WEST, EAST, INNER_SIDE[side]))
                outer = cost[j + OUTER[side], here, :] if last and t > 1 else None
                for h in range(2):
                    centre = dbuf[t - 1, h, mid, :]
                    found = jnp.minimum(
                        jnp.minimum(centre, dbuf[t - 1, h, pl.ds(c0 + PAD - 1, CH), :] + west),
                        jnp.minimum(
                            dbuf[t - 1, h, pl.ds(c0 + PAD + 1, CH), :] + east,
                            d_in[side * STEPS + t - 1, h, here, :] + inner,
                        ),
                    )
                    if not last:
                        g_out[side * STEPS + t - 1, h, here, :] = found
                        d_out[side * STEPS + t - 1, h, here, :] = centre
                    else:
                        best[h] = found if t == 1 else jnp.minimum(found, best[h] + outer)
            if last:
                for h in range(2):
                    far_out[side, h, here, :] = best[h]

        chunks(cols, ahead)

        def link(c0, side=side, within=within):
            here, mid = pl.ds(c0, CH), pl.ds(c0 + PAD, CH)
            piece = c0 // CH
            at = at_rows[side]
            inside = row_of(side, STEPS - depth + 1)
            terms = [0.0] * 4
            for h in range(2):
                dem = demand[:, half_lanes(h)]
                inv = dem * jnp.exp(temper * lab_out[side, here, half_lanes(h)])
                other = in_lab[within, here, half_lanes(h)]
                terms[0] += inv * ebuf[0, h, pl.ds(c0 + PAD - 1, CH), :]
                terms[1] += inv * ebuf[0, h, pl.ds(c0 + PAD + 1, CH), :]
                terms[2] += inv * jnp.exp(-temper * other)
                terms[3] += dem * jnp.exp(temper * other) * ebuf[0, h, mid, :]
            add_lane_sum(sums, WEST, at, piece, terms[0])
            add_lane_sum(sums, EAST, at, piece, terms[1])
            add_lane_sum(sums, INNER_SIDE[side], at, piece, terms[2])
            add_lane_sum(sums, OUTER[side], inside, piece, terms[3])

        chunks(cols, link)

    put_rows([(lab_out.at[side], labels.at[at_rows[side]]) for side in range(2)], sem)


def cross_kernel(depth, info, got1, got2, anchors, demand, path, far_in, lab, sums_in, sums, sem):
    cols = got1.shape[1]
    odd = info[1] > 0
    sums[...] = sums_in[...]

    def body(c0):
        here = pl.ds(c0, CH)
        for side in range(2):
            node0 = (info[0] + row_of(side, -depth)) * cols
            terms = 0.0
            for h in range(2):
                lanes = half_lanes(h)
                value = pick(got1, got2, odd, side, here, lanes)
                value = anchored(value, anchors[:, lanes], node0 + c0) + path[side, here, :]
                value = jnp.minimum(value, far_in[side, h, here, :])
                terms += demand[:, lanes] * jnp.exp(temper * lab[side, here, lanes]) * jnp.exp(-temper * value)
            add_lane_sum(sums, OUTER[side], row_of(side, 0), c0 // CH, terms)

    chunks(cols, body)


VM = pl.BlockSpec(memory_space=pltpu.VMEM)
SM = pl.BlockSpec(memory_space=pltpu.SMEM)
HB = pl.BlockSpec(memory_space=pltpu.HBM)


def kernel_call(body, outs, scratch, limit, specs, args, aliases=None, sems=(4,)):
    return pl.pallas_call(
        body,
        out_shape=[
            jax.ShapeDtypeStruct(shape, F32) if spec is HB else pltpu.VMEM(shape, F32) for shape, spec in outs
        ],
        in_specs=specs,
        out_specs=[spec for _, spec in outs],
        scratch_shapes=[pltpu.VMEM(s, F32) for s in scratch] + [pltpu.SemaphoreType.DMA(sems)],
        compiler_params=pltpu.CompilerParams(vmem_limit_bytes=limit),
        cost_estimate=pl.CostEstimate(flops=1 << 20, bytes_accessed=32 << 20, transcendentals=0),
        input_output_aliases=aliases or {},
    )(*(pltpu.with_memory_space_constraint(v, pltpu.HBM) if spec is HB else v for v, spec in zip(args, specs)))


def local(warm, link_costs, anchor_nodes, demand):
    rows, cols, lanes = warm.shape
    count = lax.axis_size("blk")
    me = lax.axis_index("blk")
    swaps = [[(i + a, i + 1 - a) for i in range(first, count - 1, 2) for a in (0, 1)] for first in (0, 1)]
    odd = me % 2
    own = warm

    def swap(number, message):
        return lax.ppermute(message, "blk", swaps[number])

    def cut(array, number, first, size, axis):
        low, high = first - 1, rows - first - size + 1
        start = jnp.where(odd == number, high, low)
        return lax.dynamic_slice_in_dim(array, start, size, axis)

    def lead_of(number):
        costs = cut(link_costs, number, 1, EDGE, 1)
        return jnp.concatenate([cut(warm, number, 1, 1, 0)[0], costs.reshape(-1, lanes)])

    lead = [lead_of(number) for number in range(2)]
    got_lead = [swap(number, lead[number]) for number in range(2)]
    warm, lead = lax.optimization_barrier((warm, lead))

    def exchange(first, size):
        return [swap(number, cut(warm, number, first, size, 0)) for number in range(2)]

    near = [*got_lead, *exchange(2, FIRST - 1)]
    later = [exchange(k, 1) for k in range(FIRST + 1, STEPS + 2)]
    got_costs = [m[cols:].reshape(4, EDGE, cols) for m in got_lead]
    cost_n = jnp.where(odd == 1, got_costs[0], got_costs[1])
    cost_s = jnp.where(odd == 1, got_costs[1], got_costs[0])

    row = me * rows - EDGE + jnp.arange(rows + 2 * EDGE)[:, None]
    col = jnp.arange(cols)[None, :]
    wall = jnp.stack(
        [
            jnp.broadcast_to(col == 0, (rows + 2 * EDGE, cols)),
            jnp.broadcast_to(col == cols - 1, (rows + 2 * EDGE, cols)),
            jnp.broadcast_to(row == 0, (rows + 2 * EDGE, cols)),
            jnp.broadcast_to(row == rows * count - 1, (rows + 2 * EDGE, cols)),
        ]
    )
    costs = jnp.where(wall, far_value, jnp.concatenate([cost_n, link_costs, cost_s], axis=1))
    path = jnp.stack([cost_n[NORTH].sum(axis=0), cost_s[SOUTH].sum(axis=0)])
    flat = jnp.swapaxes(costs, 0, 1).reshape(-1, cols)
    used = flat.shape[0]
    columns = jnp.pad(flat.T, ((0, 0), (0, 128 - used)))
    path_wide = jnp.broadcast_to(path[:, :, None], (2, cols, 128))
    info = jnp.stack([me * rows, odd]).astype(jnp.int32)
    anc = anchor_nodes.reshape(1, lanes)
    dem = demand.reshape(1, lanes)
    owners = lax.axis_size("org")
    width = cols // owners
    mine = lax.dynamic_slice_in_dim(costs[:, EDGE : EDGE + rows], lax.axis_index("org") * width, width, axis=2)
    scale = jnp.exp(-temper * mine) / ANCHORS
    columns, path_wide, info, anc, dem, scale = lax.optimization_barrier((columns, path_wide, info, anc, dem, scale))
    (cost,) = kernel_call(
        functools.partial(spread_kernel, used), [((used, cols, 128), VM)], [], 4 << 20, [VM], (columns,)
    )
    diag = ((2 * STEPS, 2, cols, 128), VM)
    padded = cols + 2 * PAD
    pieces = ((cols // CH, 4 * rows, CH), VM)
    whole = (warm.shape, HB)
    g, d, lab, sums, labels = kernel_call(
        first_kernel,
        [diag, diag, ((2, cols, lanes), VM), pieces, whole],
        [(rows + 2 * FIRST, 2, padded, 128)],
        9 << 20, [SM] + [HB] * 5 + [VM] * 3, (info, own, *near, anc, dem, cost),
        sems=(rows + 2 * FIRST, 2),
    )
    g, d, lab, sums, labels = kernel_call(
        functools.partial(next_kernel, FIRST + 1, False),
        [diag, diag, ((2, cols, lanes), VM), pieces, whole],
        [(STEPS, 2, padded, 128), (1, 2, padded, 128)],
        5 << 20, [SM] + [VM] * 9 + [HB], (info, *later[0], anc, dem, cost, g, d, lab, sums, labels),
        {6: 0, 7: 1, 10: 4},
    )
    far, lab, sums, labels = kernel_call(
        functools.partial(next_kernel, FIRST + 2, True),
        [((2, 2, cols, 128), VM), ((2, cols, lanes), VM), pieces, whole],
        [(STEPS, 2, padded, 128), (1, 2, padded, 128)],
        5 << 20, [SM] + [VM] * 9 + [HB], (info, *later[1], anc, dem, cost, g, d, lab, sums, labels), {10: 3},
    )
    (sums,) = kernel_call(
        functools.partial(cross_kernel, FIRST + 3),
        [pieces], [], 2 << 20, [SM] + [VM] * 8,
        (info, *later[2], anc, dem, path_wide, far, lab, sums),
    )
    total = lax.all_to_all(sums, "org", split_axis=0, concat_axis=0, tiled=True).sum(axis=0)
    return labels, total.reshape(4, rows, width) * scale


def solution(mesh):
    placed = (P("blk", None, "org"), P(None, "blk", None), P("org"), P("org"))
    return jax.shard_map(
        local,
        mesh=mesh,
        in_specs=placed,
        out_specs=(P("blk", None, "org"), P(None, "blk", "org")),
        check_vma=False,
    )
```

profile of v0, /device:TPU:6, one launch (start us, length us, event | category | flops | bytes accessed | tf_op | source)
XLA Modules:
  0.0 145.1 jit_solution(16064017818960553543)
XLA Ops:
  0.7 0.9 constant_dynamic-slice_fusion.9
  1.7 1.4 dynamic-slice_bitcast_fusion.1
  3.1 0.8 pad_maximum_fusion
  3.9 0.8 pad_maximum_fusion.1
  4.8 2.1 %constant_dynamic-slice_fusion.2 = (f32[3,512,256]{2,1,0:T(8,128)}, f32[3,512,256]{2,1,0:T(8,128)}) fusion(f32[8,512,256]{2,1,0:T(8,128)S(1)} %copy-done.2, s32[]{:T(128)S(6)} %select_n.98, s32[]{:T(128)S(6)} %select_n.97), kind=kLoop, calls=%fused_computation.12 | loop fusion | bytes 6291464 | tf_op jit(solution)/shard_map/dynamic_slice | solution.py:346
  6.8 8.6 %collective-permute-start.7 = (f32[3,512,256]{2,1,0:T(8,128)}, f32[3,512,256]{2,1,0:T(8,128)S(1)}, u32[]{:S(2)}, u32[]{:S(2)}) collective-permute-start(f32[3,512,256]{2,1,0:T(8,128)} %get-tuple-element.50), channel_id=1, source_target_pairs={{4,8},{8,4},{12,16},{16,12},{20,24},{24,20},{28,32},{32,28},{36,40... | collective-permute-start | bytes 4718600 | tf_op jit(solution)/shard_map/ppermute | solution.py:341
  15.5 0.1 collective-permute-start.6
  15.6 3.1 %collective-permute-start.1 = (f32[560,256]{1,0:T(8,128)}, f32[560,256]{1,0:T(8,128)S(1)}, u32[]{:S(2)}, u32[]{:S(2)}) collective-permute-start(f32[560,256]{1,0:T(8,128)} %pad_maximum_fusion.1), channel_id=1, source_target_pairs={{4,8},{8,4},{12,16},{16,12},{20,24},{24,20},{28,32},{32,28},{36,40... | collective-permute-start | bytes 1720328 | tf_op jit(solution)/shard_map/ppermute | solution.py:341
  18.7 0.9 collective-permute-start
  19.6 3.5 %constant_dynamic-slice_fusion = (f32[1,512,256]{2,1,0:T(8,128)}, f32[1,512,256]{2,1,0:T(8,128)}, f32[1,512,256]{2,1,0:T(8,128)}, f32[1,512,256]{2,1,0:T(8,128)}...) fusion(f32[8,512,256]{2,1,0:T(8,128)} %own.1, s32[]{:T(128)S(6)} %select_n.100, s32[]{:T(128)S(6)} %select_n.99, ...), kind=kLoop, calls=%fused_computation.10 | loop fusion | bytes 6291480 | tf_op jit(solution)/shard_map/dynamic_slice | solution.py:346
  23.1 6.5 %collective-permute-start.5 = (f32[1,512,256]{2,1,0:T(8,128)}, f32[1,512,256]{2,1,0:T(8,128)S(1)}, u32[]{:S(2)}, u32[]{:S(2)}) collective-permute-start(f32[1,512,256]{2,1,0:T(8,128)} %get-tuple-element.46), channel_id=1, source_target_pairs={{4,8},{8,4},{12,16},{16,12},{20,24},{24,20},{28,32},{32,28},{36,40... | collective-permute-start | bytes 1572872 | tf_op jit(solution)/shard_map/ppermute | solution.py:341
  29.6 0.1 pad_add_fusion.info.refs_0_
  29.7 43.9 %collective-permute-done.5.refs_2_ = f32[1,512,256]{2,1,0:T(8,128)S(1)} collective-permute-done((f32[1,512,256]{2,1,0:T(8,128)}, f32[1,512,256]{2,1,0:T(8,128)S(1)}, u32[]{:S(2)}, u32[]{:S(2)}) %collective-permute-start.5) | collective-permute-done | bytes 524320 | tf_op jit(solution)/shard_map/ppermute | solution.py:341
  73.6 8.1 %collective-permute-start.9 = (f32[1,512,256]{2,1,0:T(8,128)}, f32[1,512,256]{2,1,0:T(8,128)}, u32[]{:S(2)}, u32[]{:S(2)}) collective-permute-start(f32[1,512,256]{2,1,0:T(8,128)} %get-tuple-element.44), channel_id=1, source_target_pairs={{4,8},{8,4},{12,16},{16,12},{20,24},{24,20},{28,32},{32,28},{36,40... | collective-permute-start | bytes 1572872 | tf_op jit(solution)/shard_map/ppermute | solution.py:341
  81.8 0.1 collective-permute-start.8
  81.9 2.0 %collective-permute-start.4 = (f32[1,512,256]{2,1,0:T(8,128)}, f32[1,512,256]{2,1,0:T(8,128)}, u32[]{:S(2)}, u32[]{:S(2)}) collective-permute-start(f32[1,512,256]{2,1,0:T(8,128)} %get-tuple-element.47), channel_id=1, source_target_pairs={{0,4},{4,0},{8,12},{12,8},{16,20},{20,16},{24,28},{28,24},{32,36},... | collective-permute-start | bytes 1572872 | tf_op jit(solution)/shard_map/ppermute | solution.py:341
  83.9 2.2 %collective-permute-start.3 = (f32[1,512,256]{2,1,0:T(8,128)}, f32[1,512,256]{2,1,0:T(8,128)S(1)}, u32[]{:S(2)}, u32[]{:S(2)}) collective-permute-start(f32[1,512,256]{2,1,0:T(8,128)} %get-tuple-element.48), channel_id=1, source_target_pairs={{4,8},{8,4},{12,16},{16,12},{20,24},{24,20},{28,32},{32,28},{36,40... | collective-permute-start | bytes 1572872 | tf_op jit(solution)/shard_map/ppermute | solution.py:341
  86.1 0.1 collective-permute-start.2
  86.2 0.8 slice_select_fusion.1
  87.2 0.1 stack_broadcast_in_dim.11
  87.3 0.1 stack_broadcast_in_dim.10
  87.4 0.1 copy.11
  87.5 0.7 reshape.65
  88.3 1.0 copy.12
  89.4 0.2 broadcast_in_dim.7.path
  89.6 6.2 %shard_map.59.cost.refs_5_ = f32[80,512,128]{2,1,0:T(8,128)S(1)} custom-call(f32[512,128]{1,0:T(8,128)S(1)} %pad.4.cols_ref), custom_call_target="tpu_custom_call" | custom-call | flops 1048576 | bytes 33554432 | tf_op jit(solution)/shard_map/pallas_call | solution.py:318
  95.8 25.3 %shard_map.60 = (f32[12,2,512,128]{3,2,1,0:T(8,128)S(1)}, f32[12,2,512,128]{3,2,1,0:T(8,128)S(1)}, f32[2,512,256]{2,1,0:T(8,128)S(1)}, f32[4,32,128]{2,1,0:T(8,128)S(1)}, f32[8,512,256]{2,1,0:T(8,128)}) custom-call(s32[2]{0:T(128)S(1)} %pad_add_fusion.info.refs_0_, f32[8,512,256]{2,1,0:T(8,128)} %own.1, f32[560,256]{1,0:T(8,128)} %copy-done.5, ...), custom_call_target="tpu_custom_call" | custom-call | flops 1048576 | bytes 33554432 | tf_op jit(solution)/shard_map/pallas_call | solution.py:318
  121.2 7.3 %shard_map.61 = (f32[12,2,512,128]{3,2,1,0:T(8,128)S(1)}, f32[12,2,512,128]{3,2,1,0:T(8,128)S(1)}, f32[2,512,256]{2,1,0:T(8,128)S(1)}, f32[4,32,128]{2,1,0:T(8,128)S(1)}, f32[8,512,256]{2,1,0:T(8,128)}) custom-call(s32[2]{0:T(128)S(1)} %pad_add_fusion.info.refs_0_, ...), custom_call_target="tpu_custom_call", output_to_operand_aliasing={{0}: (6, {}), {1}: (7, {}), {4}: (10, {})} | custom-call | flops 1048576 | bytes 33554432 | tf_op jit(solution)/shard_map/pallas_call | solution.py:318
  128.5 7.0 %shard_map.62 = (f32[2,2,512,128]{3,2,1,0:T(8,128)S(1)}, f32[2,512,256]{2,1,0:T(8,128)S(1)}, f32[4,32,128]{2,1,0:T(8,128)S(1)}, f32[8,512,256]{2,1,0:T(8,128)}) custom-call(s32[2]{0:T(128)S(1)} %pad_add_fusion.info.refs_0_, f32[1,512,256]{2,1,0:T(8,128)S(1)} %collective-permute-done.2.refs_1_, ...), custom_call_target="tpu_custom_call", output_to_operand_aliasing={{3}: (10, {})} | custom-call | flops 1048576 | bytes 33554432 | tf_op jit(solution)/shard_map/pallas_call | solution.py:318
  135.6 2.1 %shard_map.63 = f32[4,32,128]{2,1,0:T(8,128)S(1)} custom-call(s32[2]{0:T(128)S(1)} %pad_add_fusion.info.refs_0_, f32[1,512,256]{2,1,0:T(8,128)} %collective-permute-done.8.got1, f32[1,512,256]{2,1,0:T(8,128)} %collective-permute-done.9.got2, s32[1,256]{1,0:T(1,128)S(1)} %bitcast.18, f32[1,256]{1,0:T(1,128)S(1)} %bitcast.22, ...), custom_call_target="tpu_custom_call" | custom-call | flops 1048576 | bytes 33554432 | tf_op jit(solution)/shard_map/pallas_call | solution.py:318
  137.7 6.8 %all_to_all.5 = f32[4,32,128]{2,1,0:T(8,128)S(1)} all-to-all(f32[4,32,128]{2,1,0:T(8,128)S(1)} %shard_map.63), channel_id=1, replica_groups=mesh['blk'=32,'org'=4] {'org'}, dimensions={0} | all-to-all | bytes 131072 | tf_op jit(solution)/shard_map/all_to_all | solution.py:421
  144.4 0.6 bitcast_multiply_fusion
  (44 shorter events, 0.3 us)
Async XLA Ops:
  1.6 3.1 %copy-start.2 = (f32[8,512,256]{2,1,0:T(8,128)S(1)}, f32[8,512,256]{2,1,0:T(8,128)}, u32[]{:S(2)}) copy-start(f32[8,512,256]{2,1,0:T(8,128)} %own.1) | copy-start | bytes 12582916
  6.8 80.5 %copy-start.6 = (f32[4,8,512]{2,1,0:T(8,128)S(1)}, f32[4,8,512]{2,1,0:T(8,128)}, u32[]{:S(2)}) copy-start(f32[4,8,512]{2,1,0:T(8,128)} %param.5) | copy-start | bytes 196612
  6.8 77.0 %collective-permute-start.7 = (f32[3,512,256]{2,1,0:T(8,128)}, f32[3,512,256]{2,1,0:T(8,128)S(1)}, u32[]{:S(2)}, u32[]{:S(2)}) collective-permute-start(f32[3,512,256]{2,1,0:T(8,128)} %get-tuple-element.50), channel_id=1, source_target_pairs={{4,8},{8,4},{12,16},{16,12},{20,24},{24,20},{28,32},{32,28},{36,40... | collective-permute-start | bytes 4718600 | tf_op jit(solution)/shard_map/ppermute | solution.py:341
  15.5 70.6 %collective-permute-start.6 = (f32[3,512,256]{2,1,0:T(8,128)}, f32[3,512,256]{2,1,0:T(8,128)}, u32[]{:S(2)}, u32[]{:S(2)}) collective-permute-start(f32[3,512,256]{2,1,0:T(8,128)} %get-tuple-element.51), channel_id=1, source_target_pairs={{0,4},{4,0},{8,12},{12,8},{16,20},{20,16},{24,28},{28,24},{32,36},... | collective-permute-start | bytes 4718600 | tf_op jit(solution)/shard_map/ppermute | solution.py:341
  15.6 66.2 %collective-permute-start.1 = (f32[560,256]{1,0:T(8,128)}, f32[560,256]{1,0:T(8,128)S(1)}, u32[]{:S(2)}, u32[]{:S(2)}) collective-permute-start(f32[560,256]{1,0:T(8,128)} %pad_maximum_fusion.1), channel_id=1, source_target_pairs={{4,8},{8,4},{12,16},{16,12},{20,24},{24,20},{28,32},{32,28},{36,40... | collective-permute-start | bytes 1720328 | tf_op jit(solution)/shard_map/ppermute | solution.py:341
  18.7 63.2 %collective-permute-start = (f32[560,256]{1,0:T(8,128)}, f32[560,256]{1,0:T(8,128)S(1)}, u32[]{:S(2)}, u32[]{:S(2)}) collective-permute-start(f32[560,256]{1,0:T(8,128)} %pad_maximum_fusion), channel_id=1, source_target_pairs={{0,4},{4,0},{8,12},{12,8},{16,20},{20,16},{24,28},{28,24},{32,36},... | collective-permute-start | bytes 1720328 | tf_op jit(solution)/shard_map/ppermute | solution.py:341
  23.1 50.5 %collective-permute-start.5 = (f32[1,512,256]{2,1,0:T(8,128)}, f32[1,512,256]{2,1,0:T(8,128)S(1)}, u32[]{:S(2)}, u32[]{:S(2)}) collective-permute-start(f32[1,512,256]{2,1,0:T(8,128)} %get-tuple-element.46), channel_id=1, source_target_pairs={{4,8},{8,4},{12,16},{16,12},{20,24},{24,20},{28,32},{32,28},{36,40... | collective-permute-start | bytes 1572872 | tf_op jit(solution)/shard_map/ppermute | solution.py:341
  73.6 62.0 %collective-permute-start.9 = (f32[1,512,256]{2,1,0:T(8,128)}, f32[1,512,256]{2,1,0:T(8,128)}, u32[]{:S(2)}, u32[]{:S(2)}) collective-permute-start(f32[1,512,256]{2,1,0:T(8,128)} %get-tuple-element.44), channel_id=1, source_target_pairs={{4,8},{8,4},{12,16},{16,12},{20,24},{24,20},{28,32},{32,28},{36,40... | collective-permute-start | bytes 1572872 | tf_op jit(solution)/shard_map/ppermute | solution.py:341
  81.8 2.1 %copy-start.4 = (f32[560,256]{1,0:T(8,128)}, f32[560,256]{1,0:T(8,128)S(1)}, u32[]{:S(2)}) copy-start(f32[560,256]{1,0:T(8,128)S(1)} %collective-permute-done.1.lead2) | copy-start | bytes 1720324
  81.8 53.8 %collective-permute-start.8 = (f32[1,512,256]{2,1,0:T(8,128)}, f32[1,512,256]{2,1,0:T(8,128)}, u32[]{:S(2)}, u32[]{:S(2)}) collective-permute-start(f32[1,512,256]{2,1,0:T(8,128)} %get-tuple-element.45), channel_id=1, source_target_pairs={{0,4},{4,0},{8,12},{12,8},{16,20},{20,16},{24,28},{28,24},{32,36},... | collective-permute-start | bytes 1572872 | tf_op jit(solution)/shard_map/ppermute | solution.py:341
  81.9 4.2 %copy-start.5 = (f32[560,256]{1,0:T(8,128)}, f32[560,256]{1,0:T(8,128)S(1)}, u32[]{:S(2)}) copy-start(f32[560,256]{1,0:T(8,128)S(1)} %collective-permute-done.lead1) | copy-start | bytes 1720324
  81.9 39.3 %collective-permute-start.4 = (f32[1,512,256]{2,1,0:T(8,128)}, f32[1,512,256]{2,1,0:T(8,128)}, u32[]{:S(2)}, u32[]{:S(2)}) collective-permute-start(f32[1,512,256]{2,1,0:T(8,128)} %get-tuple-element.47), channel_id=1, source_target_pairs={{0,4},{4,0},{8,12},{12,8},{16,20},{20,16},{24,28},{28,24},{32,36},... | collective-permute-start | bytes 1572872 | tf_op jit(solution)/shard_map/ppermute | solution.py:341
  83.9 11.9 %copy-start.3 = (f32[3,512,256]{2,1,0:T(8,128)}, f32[3,512,256]{2,1,0:T(8,128)S(1)}, u32[]{:S(2)}) copy-start(f32[3,512,256]{2,1,0:T(8,128)S(1)} %collective-permute-done.7.more2) | copy-start | bytes 4718596
  83.9 44.6 %collective-permute-start.3 = (f32[1,512,256]{2,1,0:T(8,128)}, f32[1,512,256]{2,1,0:T(8,128)S(1)}, u32[]{:S(2)}, u32[]{:S(2)}) collective-permute-start(f32[1,512,256]{2,1,0:T(8,128)} %get-tuple-element.48), channel_id=1, source_target_pairs={{4,8},{8,4},{12,16},{16,12},{20,24},{24,20},{28,32},{32,28},{36,40... | collective-permute-start | bytes 1572872 | tf_op jit(solution)/shard_map/ppermute | solution.py:341
  86.1 42.4 %collective-permute-start.2 = (f32[1,512,256]{2,1,0:T(8,128)}, f32[1,512,256]{2,1,0:T(8,128)S(1)}, u32[]{:S(2)}, u32[]{:S(2)}) collective-permute-start(f32[1,512,256]{2,1,0:T(8,128)} %get-tuple-element.49), channel_id=1, source_target_pairs={{0,4},{4,0},{8,12},{12,8},{16,20},{20,16},{24,28},{28,24},{32,36},... | collective-permute-start | bytes 1572872 | tf_op jit(solution)/shard_map/ppermute | solution.py:341
  89.6 6.2 %copy-start = (s32[256]{0:T(256)S(1)}, s32[256]{0:T(256)}, u32[]{:S(2)}) copy-start(s32[256]{0:T(256)} %param.6) | copy-start | bytes 3076
  89.6 6.2 %copy-start.1 = (f32[256]{0:T(256)S(1)}, f32[256]{0:T(256)}, u32[]{:S(2)}) copy-start(f32[256]{0:T(256)} %param.7) | copy-start | bytes 3076
where the time goes:
time: 147 us; the launch traced here: 145 us
  Pallas kernels  47.9 us (33%)
  waiting for transfers between devices  43.9 us (30%)
  starting transfers between devices  31.7 us (22%)
  local copies, waits for them, and re-layouts  10.3 us (7%)
  blocking collectives  6.76 us (5%)
  other arithmetic  3.35 us (2%)
    pallas_call x5, Pallas kernels, kernel_call(): pl.pallas_call(body, out_shape=[jax.ShapeDtypeStruct(shape, F32) if spec...  47.9 us
    ppermute x10, waiting for transfers between devices, swap(): return lax.ppermute(message, 'blk', swaps[number])  43.9 us
    ppermute x10, starting transfers between devices, swap(): return lax.ppermute(message, 'blk', swaps[number])  31.7 us
    all_to_all x1, blocking collectives, local(): lax.all_to_all(sums, 'org', split_axis=0, concat_axis=0, tiled=True)  6.76 us
    dynamic_slice x3, local copies, waits for them, and re-layouts, cut(): return lax.dynamic_slice_in_dim(array, start, size, axis)  6.54 us
  transfers between devices with their start and end apart: 10, of which 1 were waited for; matrix products, arithmetic and copies ran while one was open for 5% of the time, Pallas kernels for 32%

commit v1 on v0

--- a/solution.py
+++ b/solution.py
@@ -10,7 +10,8 @@
 ANCHORS = 1024
 STEPS = 6
 EDGE = 6
-FIRST = 4
+FIRST = 3
+SECOND = STEPS - 1 - FIRST
 PAD = 8
 CH = 128
 far_value = 1000000000.0
@@ -59,15 +60,15 @@
     sums[piece, at : at + 1, :] += jnp.sum(terms, axis=1)[None, :]
 
 
-def spread_kernel(lanes, cols_ref, out_ref, sem):
-    cols = cols_ref.shape[0]
+def spread_kernel(picks, table, out_ref, sem):
+    rest = jnp.zeros((128 - table.shape[0], CH), F32)
 
     def body(c0):
-        block = cols_ref[pl.ds(c0, CH), :]
-        for lane in range(lanes):
-            out_ref[lane, pl.ds(c0, CH), :] = jnp.broadcast_to(block[:, lane : lane + 1], (CH, 128))
-
-    chunks(cols, body)
+        block = jnp.concatenate([table[:, pl.ds(c0, CH)], rest]).T
+        for n, lane in enumerate(picks):
+            out_ref[n, pl.ds(c0, CH), :] = jnp.broadcast_to(block[:, lane : lane + 1], (CH, 128))
+
+    chunks(table.shape[1], body)
 
 
 def first_kernel(info, own, lead1, lead2, more1, more2, anchors, demand, cost, g_out, d_out, lab_out, sums, labels, buf, sem):
@@ -149,40 +150,44 @@
 
         lax.fori_loop(0, have - 2, row, 0)
 
+    done = 2 * FIRST - 4
+    first_done = STEPS - FIRST
     stores = [
-        pltpu.make_async_copy(buf.at[r, h, pl.ds(PAD, cols), :], labels.at[r + 2, :, half_lanes(h)], sem.at[r, h])
-        for r in range(4)
+        pltpu.make_async_copy(
+            buf.at[r, h, pl.ds(PAD, cols), :], labels.at[r + first_done, :, half_lanes(h)], sem.at[r, h]
+        )
+        for r in range(done)
         for h in range(2)
     ]
     for copy in stores:
         copy.start()
-    exps = 8
 
     def final(c0):
-        for r in range(4):
+        for r in range(done):
             for h in range(2):
                 value = buf[r, h, pl.ds(c0 + PAD, CH), :]
-                if r % 3 == 0:
-                    lab_out[r // 3, pl.ds(c0, CH), half_lanes(h)] = value
-                buf[r + exps, h, pl.ds(c0 + PAD, CH), :] = jnp.exp(-temper * value)
+                for n, kept in enumerate((0, done - 1)):
+                    if r == kept:
+                        lab_out[n, pl.ds(c0, CH), half_lanes(h)] = value
+                buf[r + done, h, pl.ds(c0 + PAD, CH), :] = jnp.exp(-temper * value)
 
     chunks(cols, final)
 
     def link(c0):
         piece = c0 // CH
         mid = pl.ds(c0 + PAD, CH)
-        for r in range(4):
+        for r in range(done):
             inv = [demand[:, half_lanes(h)] * jnp.exp(temper * buf[r, h, mid, :]) for h in range(2)]
 
             def add(side, shift, other, inv=inv, r=r):
-                terms = [inv[h] * buf[other + exps, h, pl.ds(c0 + PAD + shift, CH), :] for h in range(2)]
-                add_lane_sum(sums, side, r + 2, piece, terms[0] + terms[1])
+                terms = [inv[h] * buf[other + done, h, pl.ds(c0 + PAD + shift, CH), :] for h in range(2)]
+                add_lane_sum(sums, side, r + first_done, piece, terms[0] + terms[1])
 
             add(WEST, -1, r)
             add(EAST, 1, r)
             if r > 0:
                 add(NORTH, 0, r - 1)
-            if r < 3:
+            if r < done - 1:
                 add(SOUTH, 0, r + 1)
 
     chunks(cols, link)
@@ -190,20 +195,13 @@
         copy.wait()
 
 
-def pick(got1, got2, odd, side, here, lanes):
-    one, two = got1[0, here, lanes], got2[0, here, lanes]
+def pick(got1, got2, odd, side, place, here, lanes):
+    at = got1.shape[0] - 1 - place if side == 0 else place
+    one, two = got1[at, here, lanes], got2[at, here, lanes]
     return jnp.where(odd, one, two) if side == 0 else jnp.where(odd, two, one)
 
 
-def put_rows(pairs, sem):
-    copies = [pltpu.make_async_copy(src, dst, sem.at[n]) for n, (src, dst) in enumerate(pairs)]
-    for copy in copies:
-        copy.start()
-    for copy in copies:
-        copy.wait()
-
-
-def next_kernel(depth, last, *refs):
+def next_kernel(depth, place, last, *refs):
     info, got1, got2, anchors, demand, cost, g_in, d_in, in_lab, sums_in, _ = refs[:11]
     if last:
         far_out, lab_out, sums, labels, dbuf, ebuf, sem = refs[11:]
@@ -213,6 +211,7 @@
     odd = info[1] > 0
     at_rows = tuple(row_of(side, STEPS - depth) for side in range(2))
     sums[...] = sums_in[...]
+    stores = [pltpu.make_async_copy(lab_out.at[n], labels.at[at_rows[n]], sem.at[n]) for n in range(2)]
     clear_pads(dbuf, STEPS, cols)
     clear_pads(ebuf, 1, cols)
     for side in range(2):
@@ -223,7 +222,7 @@
             here, mid = pl.ds(c0, CH), pl.ds(c0 + PAD, CH)
             values = []
             for h in range(2):
-                values.append(anchored(pick(got1, got2, odd, side, here, half_lanes(h)), anchors[:, half_lanes(h)], node0 + c0))
+                values.append(anchored(pick(got1, got2, odd, side, place, here, half_lanes(h)), anchors[:, half_lanes(h)], node0 + c0))
                 dbuf[0, h, mid, :] = values[h]
             for t in range(1, STEPS + 1):
                 outer = cost[4 * cost_row(side, t - depth) + OUTER[side], here, :]
@@ -236,6 +235,7 @@
                 ebuf[0, h, mid, :] = jnp.exp(-temper * values[h])
 
         chunks(cols, chain)
+        stores[side].start()
 
         def ahead(c0, side=side):
             here, mid = pl.ds(c0, CH), pl.ds(c0 + PAD, CH)
@@ -285,7 +285,8 @@
 
         chunks(cols, link)
 
-    put_rows([(lab_out.at[side], labels.at[at_rows[side]]) for side in range(2)], sem)
+    for copy in stores:
+        copy.wait()
 
 
 def cross_kernel(depth, info, got1, got2, anchors, demand, path, far_in, lab, sums_in, sums, sem):
@@ -300,7 +301,7 @@
             terms = 0.0
             for h in range(2):
                 lanes = half_lanes(h)
-                value = pick(got1, got2, odd, side, here, lanes)
+                value = pick(got1, got2, odd, side, 0, here, lanes)
                 value = anchored(value, anchors[:, lanes], node0 + c0) + path[side, here, :]
                 value = jnp.minimum(value, far_in[side, h, here, :])
                 terms += demand[:, lanes] * jnp.exp(temper * lab[side, here, lanes]) * jnp.exp(-temper * value)
@@ -346,9 +347,10 @@
         return lax.dynamic_slice_in_dim(array, start, size, axis)
 
     def lead_of(number):
-        costs = cut(link_costs, number, 1, EDGE, 1)
-        return jnp.concatenate([cut(warm, number, 1, 1, 0)[0], costs.reshape(-1, lanes)])
-
+        parts = [flat_costs[:, n : n + lanes] for n in range(0, cols, lanes)]
+        return jnp.concatenate([cut(warm, number, 1, 1, 0)[0], *parts])
+
+    flat_costs = link_costs.reshape(4 * rows, cols)
     lead = [lead_of(number) for number in range(2)]
     got_lead = [swap(number, lead[number]) for number in range(2)]
     warm, lead = lax.optimization_barrier((warm, lead))
@@ -357,37 +359,44 @@
         return [swap(number, cut(warm, number, first, size, 0)) for number in range(2)]
 
     near = [*got_lead, *exchange(2, FIRST - 1)]
-    later = [exchange(k, 1) for k in range(FIRST + 1, STEPS + 2)]
-    got_costs = [m[cols:].reshape(4, EDGE, cols) for m in got_lead]
-    cost_n = jnp.where(odd == 1, got_costs[0], got_costs[1])
-    cost_s = jnp.where(odd == 1, got_costs[1], got_costs[0])
-
-    row = me * rows - EDGE + jnp.arange(rows + 2 * EDGE)[:, None]
+    later = {k: exchange(k, SECOND if k == FIRST + 1 else 1) for k in (FIRST + 1, STEPS, STEPS + 1)}
+    got_costs = [
+        jnp.concatenate([m[n : n + 4 * rows] for n in range(cols, m.shape[0], 4 * rows)], axis=1) for m in got_lead
+    ]
+    cost_n = jnp.where(odd == 1, got_costs[0], got_costs[1]).reshape(4, rows, cols)
+    cost_s = jnp.where(odd == 1, got_costs[1], got_costs[0]).reshape(4, rows, cols)
+
+    row = (me * rows + jnp.arange(rows))[:, None]
     col = jnp.arange(cols)[None, :]
+    wide = (rows, cols)
     wall = jnp.stack(
         [
-            jnp.broadcast_to(col == 0, (rows + 2 * EDGE, cols)),
-            jnp.broadcast_to(col == cols - 1, (rows + 2 * EDGE, cols)),
-            jnp.broadcast_to(row == 0, (rows + 2 * EDGE, cols)),
-            jnp.broadcast_to(row == rows * count - 1, (rows + 2 * EDGE, cols)),
+            jnp.broadcast_to(col == 0, wide),
+            jnp.broadcast_to(col == cols - 1, wide),
+            jnp.broadcast_to(row == 0, wide),
+            jnp.broadcast_to(row == rows * count - 1, wide),
         ]
     )
-    costs = jnp.where(wall, far_value, jnp.concatenate([cost_n, link_costs, cost_s], axis=1))
-    path = jnp.stack([cost_n[NORTH].sum(axis=0), cost_s[SOUTH].sum(axis=0)])
-    flat = jnp.swapaxes(costs, 0, 1).reshape(-1, cols)
-    used = flat.shape[0]
-    columns = jnp.pad(flat.T, ((0, 0), (0, 128 - used)))
+    own_costs = jnp.where(wall, far_value, link_costs)
+    sides = ((col == 0)[None], (col == cols - 1)[None])
+    cost_n, cost_s = (
+        jnp.concatenate([*(jnp.where(w, far_value, c[k : k + 1]) for k, w in enumerate(sides)), c[2:]]) for c in (cost_n, cost_s)
+    )
+    path = jnp.stack([cost_n[NORTH, rows - EDGE :].sum(axis=0), cost_s[SOUTH, :EDGE].sum(axis=0)])
+    table = jnp.concatenate([cost_n, own_costs, cost_s], axis=1).reshape(-1, cols)
+    total = 3 * rows
+    used = [k * total + r for r in range(rows - EDGE, 2 * rows + EDGE) for k in range(4)]
     path_wide = jnp.broadcast_to(path[:, :, None], (2, cols, 128))
     info = jnp.stack([me * rows, odd]).astype(jnp.int32)
     anc = anchor_nodes.reshape(1, lanes)
     dem = demand.reshape(1, lanes)
     owners = lax.axis_size("org")
     width = cols // owners
-    mine = lax.dynamic_slice_in_dim(costs[:, EDGE : EDGE + rows], lax.axis_index("org") * width, width, axis=2)
+    mine = lax.dynamic_slice_in_dim(own_costs, lax.axis_index("org") * width, width, axis=2)
     scale = jnp.exp(-temper * mine) / ANCHORS
-    columns, path_wide, info, anc, dem, scale = lax.optimization_barrier((columns, path_wide, info, anc, dem, scale))
+    table, path_wide, info, anc, dem, scale = lax.optimization_barrier((table, path_wide, info, anc, dem, scale))
     (cost,) = kernel_call(
-        functools.partial(spread_kernel, used), [((used, cols, 128), VM)], [], 4 << 20, [VM], (columns,)
+        functools.partial(spread_kernel, used), [((len(used), cols, 128), VM)], [], 1 << 20, [VM], (table,)
     )
     diag = ((2 * STEPS, 2, cols, 128), VM)
     padded = cols + 2 * PAD
@@ -397,26 +406,29 @@
         first_kernel,
         [diag, diag, ((2, cols, lanes), VM), pieces, whole],
         [(rows + 2 * FIRST, 2, padded, 128)],
-        9 << 20, [SM] + [HB] * 5 + [VM] * 3, (info, own, *near, anc, dem, cost),
+        7680 << 10, [SM] + [HB] * 5 + [VM] * 3, (info, own, *near, anc, dem, cost),
         sems=(rows + 2 * FIRST, 2),
     )
-    g, d, lab, sums, labels = kernel_call(
-        functools.partial(next_kernel, FIRST + 1, False),
-        [diag, diag, ((2, cols, lanes), VM), pieces, whole],
-        [(STEPS, 2, padded, 128), (1, 2, padded, 128)],
-        5 << 20, [SM] + [VM] * 9 + [HB], (info, *later[0], anc, dem, cost, g, d, lab, sums, labels),
-        {6: 0, 7: 1, 10: 4},
-    )
+    for place in range(SECOND):
+        depth = FIRST + 1 + place
+        g, d, lab, sums, labels = kernel_call(
+            functools.partial(next_kernel, depth, place, False),
+            [diag, diag, ((2, cols, lanes), VM), pieces, whole],
+            [(STEPS, 2, padded, 128), (1, 2, padded, 128)],
+            5 << 20, [SM] + [VM] * 9 + [HB],
+            (info, *later[FIRST + 1], anc, dem, cost, g, d, lab, sums, labels),
+            {6: 0, 7: 1, 10: 4},
+        )
     far, lab, sums, labels = kernel_call(
-        functools.partial(next_kernel, FIRST + 2, True),
+        functools.partial(next_kernel, STEPS, 0, True),
         [((2, 2, cols, 128), VM), ((2, cols, lanes), VM), pieces, whole],
         [(STEPS, 2, padded, 128), (1, 2, padded, 128)],
-        5 << 20, [SM] + [VM] * 9 + [HB], (info, *later[1], anc, dem, cost, g, d, lab, sums, labels), {10: 3},
+        5 << 20, [SM] + [VM] * 9 + [HB], (info, *later[STEPS], anc, dem, cost, g, d, lab, sums, labels), {10: 3},
     )
     (sums,) = kernel_call(
-        functools.partial(cross_kernel, FIRST + 3),
+        functools.partial(cross_kernel, STEPS + 1),
         [pieces], [], 2 << 20, [SM] + [VM] * 8,
-        (info, *later[2], anc, dem, path_wide, far, lab, sums),
+        (info, *later[STEPS + 1], anc, dem, path_wide, far, lab, sums),
     )
     total = lax.all_to_all(sums, "org", split_axis=0, concat_axis=0, tiled=True).sum(axis=0)
     return labels, total.reshape(4, rows, width) * scale

time: 147 us -> 124 us (0.84)
  waiting for transfers between devices: 43.9 us -> 25.5 us
  Pallas kernels: 47.9 us -> 41.9 us
  starting transfers between devices: 31.7 us -> 37.6 us
  local copies, waits for them, and re-layouts: 10.3 us -> 8.76 us
    ppermute x10, waiting for transfers between devices: 43.9 us -> 25.5 us  [swap(): return lax.ppermute(message, 'blk', swaps[number])]
    pallas_call x5 -> x6, Pallas kernels: 47.9 us -> 41.9 us  [kernel_call(): pl.pallas_call(body, out_shape=[jax.ShapeDtypeStruct(shape, F32) if spec...]
    ppermute x10, starting transfers between devices: 31.7 us -> 37.6 us  [swap(): return lax.ppermute(message, 'blk', swaps[number])]
    slice x5 -> x4, local copies, waits for them, and re-layouts: 0.03 us -> 2.35 us  [the longest x2 1.56 us: local(): m[n:n + 4 * rows]]
    reshape x4 -> x0, local copies, waits for them, and re-layouts: 1.79 us -> none  [the longest x2 1.76 us: local(): flat = jnp.swapaxes(costs, 0, 1).reshape(-1, cols)]
    dynamic_slice x3 -> x2, local copies, waits for them, and re-layouts: 6.54 us -> 4.77 us  [cut(): return lax.dynamic_slice_in_dim(array, start, size, axis)]
  transfers between devices with their start and end apart: 10 -> 10, of which waited for: 1 -> 2; matrix products, arithmetic and copies ran while one was open for 5% -> 6% of each run, Pallas kernels for 32% -> 33%
where the time goes in v1:
time: 124 us; the launch traced here: 123 us
  Pallas kernels  41.9 us (34%)
  starting transfers between devices  37.6 us (30%)
  waiting for transfers between devices  25.5 us (21%)
  local copies, waits for them, and re-layouts  8.76 us (7%)
  blocking collectives  6.49 us (5%)
  other arithmetic  1.93 us (2%)
    pallas_call x6, Pallas kernels, kernel_call(): pl.pallas_call(body, out_shape=[jax.ShapeDtypeStruct(shape, F32) if spec...  41.9 us
    ppermute x10, starting transfers between devices, swap(): return lax.ppermute(message, 'blk', swaps[number])  37.6 us
    ppermute x10, waiting for transfers between devices, swap(): return lax.ppermute(message, 'blk', swaps[number])  25.5 us
    all_to_all x1, blocking collectives, local(): lax.all_to_all(sums, 'org', split_axis=0, concat_axis=0, tiled=True)  6.49 us
    dynamic_slice x2, local copies, waits for them, and re-layouts, cut(): return lax.dynamic_slice_in_dim(array, start, size, axis)  4.77 us
  transfers between devices with their start and end apart: 10, of which 2 were waited for; matrix products, arithmetic and copies ran while one was open for 6% of the time, Pallas kernels for 33%

profile of v1, /device:TPU:6, one launch (start us, length us, event | category | flops | bytes accessed | tf_op | source)
XLA Modules:
  0.0 123.1 jit_solution(1097059470362029568)
XLA Ops:
  0.7 0.8 fusion.10
  1.4 1.3 %dynamic-slice_bitcast_fusion.1 = (f32[512,256]{1,0:T(8,128)S(1)}, f32[512,256]{1,0:T(8,128)S(1)}) fusion(f32[8,512,256]{2,1,0:T(8,128)} %own.1, s32[]{:T(128)S(6)} %select_n.90, s32[]{:T(128)S(6)} %select_n.91), kind=kLoop, calls=%fused_computation.5 | loop fusion | bytes 2097160 | tf_op jit(solution)/shard_map/squeeze | solution.py:351
  2.7 1.1 pad_maximum_fusion.1
  3.8 1.6 %collective-permute-start = (f32[576,256]{1,0:T(8,128)}, f32[576,256]{1,0:T(8,128)}, u32[]{:S(2)}, u32[]{:S(2)}) collective-permute-start(f32[576,256]{1,0:T(8,128)} %get-tuple-element.73), channel_id=1, source_target_pairs={{0,4},{4,0},{8,12},{12,8},{16,20},{20,16},{24,28},{28,24},{32,36},... | collective-permute-start | bytes 1769480 | tf_op jit(solution)/shard_map/ppermute | solution.py:342
  5.4 7.7 %collective-permute-start.1 = (f32[576,256]{1,0:T(8,128)}, f32[576,256]{1,0:T(8,128)}, u32[]{:S(2)}, u32[]{:S(2)}) collective-permute-start(f32[576,256]{1,0:T(8,128)} %get-tuple-element.74), channel_id=1, source_target_pairs={{4,8},{8,4},{12,16},{16,12},{20,24},{24,20},{28,32},{32,28},{36,40... | collective-permute-start | bytes 1769480 | tf_op jit(solution)/shard_map/ppermute | solution.py:342
  13.1 3.1 %constant_dynamic-slice_fusion.2 = (f32[2,512,256]{2,1,0:T(8,128)S(1)}, f32[2,512,256]{2,1,0:T(8,128)}, f32[2,512,256]{2,1,0:T(8,128)S(1)}) fusion(f32[8,512,256]{2,1,0:T(8,128)} %own.1, s32[]{:T(128)S(6)} %select_n.107, s32[]{:T(128)S(6)} %select_n.106), kind=kLoop, calls=%fused_computation.29 | loop fusion | bytes 6291464 | tf_op jit(solution)/shard_map/dynamic_slice | solution.py:347
  16.2 3.2 %collective-permute-start.7 = (f32[2,512,256]{2,1,0:T(8,128)S(1)}, f32[2,512,256]{2,1,0:T(8,128)}, u32[]{:S(2)}, u32[]{:S(2)}) collective-permute-start(f32[2,512,256]{2,1,0:T(8,128)S(1)} %get-tuple-element.58), channel_id=1, source_target_pairs={{4,8},{8,4},{12,16},{16,12},{20,24},{24,20},{28,32},{32,28},{36,40... | collective-permute-start | bytes 3145736 | tf_op jit(solution)/shard_map/ppermute | solution.py:342
  19.4 1.0 collective-permute-start.4
  20.4 0.1 stack_broadcast_in_dim.10
  20.5 0.1 stack_broadcast_in_dim.11
  20.6 0.1 pad_add_fusion.info.refs_0_
  20.7 1.7 %constant_dynamic-slice_fusion = (f32[1,512,256]{2,1,0:T(8,128)S(1)}, f32[1,512,256]{2,1,0:T(8,128)S(1)}, f32[1,512,256]{2,1,0:T(8,128)S(1)}, f32[1,512,256]{2,1,0:T(8,128)S(1)}) fusion(f32[8,512,256]{2,1,0:T(8,128)} %own.1, s32[]{:T(128)S(6)} %select_n.109, s32[]{:T(128)S(6)} %select_n.108, s32[]{:T(128)S(6)} %select_n.105, s32[]{:T(128)S(6)} %select_n.104), kind=kLoop, calls=%fused_computation.27 | loop fusion | bytes 4194320 | tf_op jit(solution)/shard_map/dynamic_slice | solution.py:347
  22.4 6.5 %collective-permute-start.5 = (f32[2,512,256]{2,1,0:T(8,128)S(1)}, f32[2,512,256]{2,1,0:T(8,128)S(1)}, u32[]{:S(2)}, u32[]{:S(2)}) collective-permute-start(f32[2,512,256]{2,1,0:T(8,128)S(1)} %get-tuple-element.60), channel_id=1, source_target_pairs={{4,8},{8,4},{12,16},{16,12},{20,24},{24,20},{28,32},{32,28},{36,40... | collective-permute-start | bytes 3145736 | tf_op jit(solution)/shard_map/ppermute | solution.py:342
  28.8 0.8 fusion.8
  29.6 0.1 collective-permute-start.2
  29.7 0.8 fusion.9
  30.6 12.0 %collective-permute-done.6.more1 = f32[2,512,256]{2,1,0:T(8,128)} collective-permute-done((f32[2,512,256]{2,1,0:T(8,128)}, f32[2,512,256]{2,1,0:T(8,128)}, u32[]{:S(2)}, u32[]{:S(2)}) %collective-permute-start.6) | collective-permute-done | bytes 1048608 | tf_op jit(solution)/shard_map/ppermute | solution.py:342
  42.5 8.8 %collective-permute-start.3 = (f32[1,512,256]{2,1,0:T(8,128)S(1)}, f32[1,512,256]{2,1,0:T(8,128)S(1)}, u32[]{:S(2)}, u32[]{:S(2)}) collective-permute-start(f32[1,512,256]{2,1,0:T(8,128)S(1)} %get-tuple-element.56), channel_id=1, source_target_pairs={{4,8},{8,4},{12,16},{16,12},{20,24},{24,20},{28,32},{32,28},{36,40... | collective-permute-start | bytes 1572872 | tf_op jit(solution)/shard_map/ppermute | solution.py:342
  51.3 0.1 collective-permute-start.8
  51.4 13.5 %collective-permute-done.4.refs_1_ = f32[2,512,256]{2,1,0:T(8,128)S(1)} collective-permute-done((f32[2,512,256]{2,1,0:T(8,128)S(1)}, f32[2,512,256]{2,1,0:T(8,128)S(1)}, u32[]{:S(2)}, u32[]{:S(2)}) %collective-permute-start.4) | collective-permute-done | bytes 1048608 | tf_op jit(solution)/shard_map/ppermute | solution.py:342
  64.9 8.8 %collective-permute-start.9 = (f32[1,512,256]{2,1,0:T(8,128)S(1)}, f32[1,512,256]{2,1,0:T(8,128)S(1)}, u32[]{:S(2)}, u32[]{:S(2)}) collective-permute-start(f32[1,512,256]{2,1,0:T(8,128)S(1)} %get-tuple-element.54), channel_id=1, source_target_pairs={{4,8},{8,4},{12,16},{16,12},{20,24},{24,20},{28,32},{32,28},{36,40... | collective-permute-start | bytes 1572872 | tf_op jit(solution)/shard_map/ppermute | solution.py:342
  73.8 0.2 broadcast_in_dim.48.path
  74.0 0.0 copy-start
  74.0 0.0 copy-start.1
  74.0 6.7 %shard_map.59.cost.refs_5_ = f32[80,512,128]{2,1,0:T(8,128)S(1)} custom-call(f32[96,512]{1,0:T(8,128)S(1)} %bitcast.26), custom_call_target="tpu_custom_call" | custom-call | flops 1048576 | bytes 33554432 | tf_op jit(solution)/shard_map/pallas_call | solution.py:319
  80.7 17.2 %shard_map.60 = (f32[12,2,512,128]{3,2,1,0:T(8,128)S(1)}, f32[12,2,512,128]{3,2,1,0:T(8,128)S(1)}, f32[2,512,256]{2,1,0:T(8,128)S(1)}, f32[4,32,128]{2,1,0:T(8,128)S(1)}, f32[8,512,256]{2,1,0:T(8,128)}) custom-call(s32[2]{0:T(128)S(1)} %pad_add_fusion.info.refs_0_, f32[8,512,256]{2,1,0:T(8,128)} %own.1, f32[576,256]{1,0:T(8,128)} %collective-permute-done.lead1, ...), custom_call_target="tpu_custom_call" | custom-call | flops 1048576 | bytes 33554432 | tf_op jit(solution)/shard_map/pallas_call | solution.py:319
  97.9 5.6 %shard_map.61 = (f32[12,2,512,128]{3,2,1,0:T(8,128)S(1)}, f32[12,2,512,128]{3,2,1,0:T(8,128)S(1)}, f32[2,512,256]{2,1,0:T(8,128)S(1)}, f32[4,32,128]{2,1,0:T(8,128)S(1)}, f32[8,512,256]{2,1,0:T(8,128)}) custom-call(s32[2]{0:T(128)S(1)} %pad_add_fusion.info.refs_0_, ...), custom_call_target="tpu_custom_call", output_to_operand_aliasing={{0}: (6, {}), {1}: (7, {}), {4}: (10, {})} | custom-call | flops 1048576 | bytes 33554432 | tf_op jit(solution)/shard_map/pallas_call | solution.py:319
  103.6 5.6 %shard_map.62 = (f32[12,2,512,128]{3,2,1,0:T(8,128)S(1)}, f32[12,2,512,128]{3,2,1,0:T(8,128)S(1)}, f32[2,512,256]{2,1,0:T(8,128)S(1)}, f32[4,32,128]{2,1,0:T(8,128)S(1)}, f32[8,512,256]{2,1,0:T(8,128)}) custom-call(s32[2]{0:T(128)S(1)} %pad_add_fusion.info.refs_0_, ...), custom_call_target="tpu_custom_call", output_to_operand_aliasing={{0}: (6, {}), {1}: (7, {}), {4}: (10, {})} | custom-call | flops 1048576 | bytes 33554432 | tf_op jit(solution)/shard_map/pallas_call | solution.py:319
  109.2 5.3 %shard_map.63 = (f32[2,2,512,128]{3,2,1,0:T(8,128)S(1)}, f32[2,512,256]{2,1,0:T(8,128)S(1)}, f32[4,32,128]{2,1,0:T(8,128)S(1)}, f32[8,512,256]{2,1,0:T(8,128)}) custom-call(s32[2]{0:T(128)S(1)} %pad_add_fusion.info.refs_0_, f32[1,512,256]{2,1,0:T(8,128)S(1)} %collective-permute-done.2.refs_1_, ...), custom_call_target="tpu_custom_call", output_to_operand_aliasing={{3}: (10, {})} | custom-call | flops 1048576 | bytes 33554432 | tf_op jit(solution)/shard_map/pallas_call | solution.py:319
  114.5 1.4 %shard_map.64 = f32[4,32,128]{2,1,0:T(8,128)S(1)} custom-call(s32[2]{0:T(128)S(1)} %pad_add_fusion.info.refs_0_, f32[1,512,256]{2,1,0:T(8,128)S(1)} %collective-permute-done.8.got1, f32[1,512,256]{2,1,0:T(8,128)S(1)} %collective-permute-done.9.got2, s32[1,256]{1,0:T(1,128)S(1)} %bitcast.31, f32[1,256]{1,0:T(1,128)S(1)} %bitcast.36, ...), custom_call_target="tpu_custom_call" | custom-call | flops 1048576 | bytes 33554432 | tf_op jit(solution)/shard_map/pallas_call | solution.py:319
  116.0 6.5 %all_to_all.5 = f32[4,32,128]{2,1,0:T(8,128)S(1)} all-to-all(f32[4,32,128]{2,1,0:T(8,128)S(1)} %shard_map.64), channel_id=1, replica_groups=mesh['blk'=32,'org'=4] {'org'}, dimensions={0} | all-to-all | bytes 131072 | tf_op jit(solution)/shard_map/all_to_all | solution.py:433
  122.5 0.6 bitcast_multiply_fusion
  (27 shorter events, 0.2 us)
Async XLA Ops:
  2.7 17.9 %copy-start.2 = (f32[4,8,512]{2,1,0:T(8,128)S(1)}, f32[4,8,512]{2,1,0:T(8,128)}, u32[]{:S(2)}) copy-start(f32[4,8,512]{2,1,0:T(8,128)} %param.5) | copy-start | bytes 196612
  3.8 18.5 %collective-permute-start = (f32[576,256]{1,0:T(8,128)}, f32[576,256]{1,0:T(8,128)}, u32[]{:S(2)}, u32[]{:S(2)}) collective-permute-start(f32[576,256]{1,0:T(8,128)} %get-tuple-element.73), channel_id=1, source_target_pairs={{0,4},{4,0},{8,12},{12,8},{16,20},{20,16},{24,28},{28,24},{32,36},... | collective-permute-start | bytes 1769480 | tf_op jit(solution)/shard_map/ppermute | solution.py:342
  5.4 24.2 %collective-permute-start.1 = (f32[576,256]{1,0:T(8,128)}, f32[576,256]{1,0:T(8,128)}, u32[]{:S(2)}, u32[]{:S(2)}) collective-permute-start(f32[576,256]{1,0:T(8,128)} %get-tuple-element.74), channel_id=1, source_target_pairs={{4,8},{8,4},{12,16},{16,12},{20,24},{24,20},{28,32},{32,28},{36,40... | collective-permute-start | bytes 1769480 | tf_op jit(solution)/shard_map/ppermute | solution.py:342
  16.2 26.3 %collective-permute-start.6 = (f32[2,512,256]{2,1,0:T(8,128)}, f32[2,512,256]{2,1,0:T(8,128)}, u32[]{:S(2)}, u32[]{:S(2)}) collective-permute-start(f32[2,512,256]{2,1,0:T(8,128)} %get-tuple-element.59), channel_id=1, source_target_pairs={{0,4},{4,0},{8,12},{12,8},{16,20},{20,16},{24,28},{28,24},{32,36},... | collective-permute-start | bytes 3145736 | tf_op jit(solution)/shard_map/ppermute | solution.py:342
  16.2 35.1 %collective-permute-start.7 = (f32[2,512,256]{2,1,0:T(8,128)S(1)}, f32[2,512,256]{2,1,0:T(8,128)}, u32[]{:S(2)}, u32[]{:S(2)}) collective-permute-start(f32[2,512,256]{2,1,0:T(8,128)S(1)} %get-tuple-element.58), channel_id=1, source_target_pairs={{4,8},{8,4},{12,16},{16,12},{20,24},{24,20},{28,32},{32,28},{36,40... | collective-permute-start | bytes 3145736 | tf_op jit(solution)/shard_map/ppermute | solution.py:342
  19.4 45.5 %collective-permute-start.4 = (f32[2,512,256]{2,1,0:T(8,128)S(1)}, f32[2,512,256]{2,1,0:T(8,128)S(1)}, u32[]{:S(2)}, u32[]{:S(2)}) collective-permute-start(f32[2,512,256]{2,1,0:T(8,128)S(1)} %get-tuple-element.60), channel_id=1, source_target_pairs={{0,4},{4,0},{8,12},{12,8},{16,20},{20,16},{24,28},{28,24},{32,36},... | collective-permute-start | bytes 3145736 | tf_op jit(solution)/shard_map/ppermute | solution.py:342
  22.4 75.6 %collective-permute-start.5 = (f32[2,512,256]{2,1,0:T(8,128)S(1)}, f32[2,512,256]{2,1,0:T(8,128)S(1)}, u32[]{:S(2)}, u32[]{:S(2)}) collective-permute-start(f32[2,512,256]{2,1,0:T(8,128)S(1)} %get-tuple-element.60), channel_id=1, source_target_pairs={{4,8},{8,4},{12,16},{16,12},{20,24},{24,20},{28,32},{32,28},{36,40... | collective-permute-start | bytes 3145736 | tf_op jit(solution)/shard_map/ppermute | solution.py:342
  29.6 79.6 %collective-permute-start.2 = (f32[1,512,256]{2,1,0:T(8,128)S(1)}, f32[1,512,256]{2,1,0:T(8,128)S(1)}, u32[]{:S(2)}, u32[]{:S(2)}) collective-permute-start(f32[1,512,256]{2,1,0:T(8,128)S(1)} %get-tuple-element.57), channel_id=1, source_target_pairs={{0,4},{4,0},{8,12},{12,8},{16,20},{20,16},{24,28},{28,24},{32,36},... | collective-permute-start | bytes 1572872 | tf_op jit(solution)/shard_map/ppermute | solution.py:342
  42.5 66.7 %collective-permute-start.3 = (f32[1,512,256]{2,1,0:T(8,128)S(1)}, f32[1,512,256]{2,1,0:T(8,128)S(1)}, u32[]{:S(2)}, u32[]{:S(2)}) collective-permute-start(f32[1,512,256]{2,1,0:T(8,128)S(1)} %get-tuple-element.56), channel_id=1, source_target_pairs={{4,8},{8,4},{12,16},{16,12},{20,24},{24,20},{28,32},{32,28},{36,40... | collective-permute-start | bytes 1572872 | tf_op jit(solution)/shard_map/ppermute | solution.py:342
  51.3 63.2 %collective-permute-start.8 = (f32[1,512,256]{2,1,0:T(8,128)S(1)}, f32[1,512,256]{2,1,0:T(8,128)S(1)}, u32[]{:S(2)}, u32[]{:S(2)}) collective-permute-start(f32[1,512,256]{2,1,0:T(8,128)S(1)} %get-tuple-element.55), channel_id=1, source_target_pairs={{0,4},{4,0},{8,12},{12,8},{16,20},{20,16},{24,28},{28,24},{32,36},... | collective-permute-start | bytes 1572872 | tf_op jit(solution)/shard_map/ppermute | solution.py:342
  64.9 49.6 %collective-permute-start.9 = (f32[1,512,256]{2,1,0:T(8,128)S(1)}, f32[1,512,256]{2,1,0:T(8,128)S(1)}, u32[]{:S(2)}, u32[]{:S(2)}) collective-permute-start(f32[1,512,256]{2,1,0:T(8,128)S(1)} %get-tuple-element.54), channel_id=1, source_target_pairs={{4,8},{8,4},{12,16},{16,12},{20,24},{24,20},{28,32},{32,28},{36,40... | collective-permute-start | bytes 1572872 | tf_op jit(solution)/shard_map/ppermute | solution.py:342
  74.0 6.7 %copy-start = (s32[256]{0:T(256)S(1)}, s32[256]{0:T(256)}, u32[]{:S(2)}) copy-start(s32[256]{0:T(256)} %param.6) | copy-start | bytes 3076
  74.0 6.7 %copy-start.1 = (f32[256]{0:T(256)S(1)}, f32[256]{0:T(256)}, u32[]{:S(2)}) copy-start(f32[256]{0:T(256)} %param.7) | copy-start | bytes 3076
